TPU v7x, 128 devices: a whole 4x4x4 slice. The times are simulated.
128 devices in a mesh: seq: 16 (over y_lo, x, core), tp: 8 (over y_hi, z).
Axes of the slice: x: 4, y: 4 (y_hi: 2, y_lo: 2; y = y_hi * 2 + y_lo), z: 4, core: 2. Of those that a mesh axis runs over, the one named last changes fastest.
Arguments:
- queries: bfloat16 [8192, 6144], P('seq', 'tp'), may hold values from -6 to 6
- keys: bfloat16 [8192, 1024], P('seq', 'tp'), may hold values from -6 to 6
- values: bfloat16 [8192, 1024], P('seq', 'tp'), may hold values from -6 to 6
- segment_ids: int32 [8192], replicated, may hold values from 0 to 7, never falling along the last dimension, each value on 1 to 6144 neighbouring positions
- packing: int32 [64, 2], replicated, may hold values from 0 to 15, as said below
- out_weight: bfloat16 [6144, 12288], P('tp', 'seq'), may hold values from -0.625 to 0.625
Outputs:
- attended: bfloat16 [8192, 12288], P('seq', 'tp')
Inputs may be any that keep to these rules, and one draw needn't show every extreme that they name: `packing`: each arriving block gets a distinct packed place, so every packed shard receives exactly 4 blocks at offsets 0 to 3; the blocks of one shard go to 4 different packed shards. `segment_ids`: document ids never fall along the tokens; each document has 1 to 6144 tokens and one has exactly 6144.
All inputs are finite; a program needn't handle non-finite values.
Results may differ from a plain program's by a relative error of at most 0.015.
Values may be sent and summed in bfloat16 or wider, within the bound.
A program may use at most 128 MiB of HBM per device.

v0:
```python
import functools
import math
import jax
import jax.numpy as jnp
from jax import lax
from jax.sharding import Mesh, PartitionSpec as P

HEAD_DIM = 128
WINDOW = 4096
BLOCK = 128
SEQ = ("ylo", "x", "c")
TP = ("yhi", "z")


def attend_head(q_rows, k_rows, v_rows, q_pos, k_pos, q_seg, k_seg):
    scores = lax.dot_general(
        q_rows, k_rows, (((1,), (1,)), ((), ())), preferred_element_type=jnp.float32
    )
    scores = scores * (1.0 / math.sqrt(HEAD_DIM))
    allowed = (k_pos[None, :] <= q_pos[:, None]) & (k_pos[None, :] > q_pos[:, None] - WINDOW)
    allowed = allowed & (k_seg[None, :] == q_seg[:, None])
    scores = jnp.where(allowed, scores, -jnp.inf)
    top_score = jnp.max(scores, axis=1, keepdims=True)
    expo = jnp.exp(scores - top_score)
    weights = (expo / jnp.sum(expo, axis=1, keepdims=True)).astype(jnp.bfloat16)
    return jnp.dot(weights, v_rows, preferred_element_type=jnp.float32).astype(jnp.bfloat16)


def shards(seq_count, queries, keys, values, segment_ids, packing, out_weight):
    tok_rows = queries.shape[0]
    q_cols = queries.shape[1]
    kv_cols = keys.shape[1]
    shard_index = lax.axis_index(SEQ)
    per_shard = tok_rows // BLOCK
    blocks_all = packing.shape[0]
    kv_local = jnp.concatenate([keys, values], axis=1)
    kv_all = lax.all_gather(kv_local, SEQ, axis=0, tiled=True)
    kv_blocks = kv_all.reshape(blocks_all, BLOCK, 2 * kv_cols)
    target = packing[:, 0] * per_shard + packing[:, 1]
    source = (
        jnp.zeros((blocks_all,), jnp.int32).at[target].set(jnp.arange(blocks_all, dtype=jnp.int32))
    )
    span_blocks = WINDOW // BLOCK
    ctx_blocks = span_blocks + per_shard
    blk_ids = shard_index * per_shard - span_blocks + jnp.arange(ctx_blocks, dtype=jnp.int32)
    src = jnp.take(source, jnp.clip(blk_ids, 0, blocks_all - 1))
    context = jnp.take(kv_blocks, src, axis=0).reshape(ctx_blocks * BLOCK, 2 * kv_cols)
    own_blocks = queries.reshape(per_shard, BLOCK, q_cols)
    own_list = lax.dynamic_slice_in_dim(packing, shard_index * per_shard, per_shard, 0)
    slot_ids = jnp.arange(seq_count, dtype=jnp.int32)
    routing = (own_list[:, 0][None, :] == slot_ids[:, None]).astype(jnp.bfloat16)
    outgoing = jnp.einsum(
        "db,brc->drc", routing, own_blocks, preferred_element_type=jnp.float32
    ).astype(jnp.bfloat16)
    incoming = lax.all_to_all(outgoing, SEQ, split_axis=0, concat_axis=0, tiled=True)
    arriving = packing[:, 0] == shard_index
    offset_ids = jnp.arange(per_shard, dtype=jnp.int32)
    at_offset = ((packing[:, 1][None, :] == offset_ids[:, None]) & arriving[None, :]).astype(
        jnp.float32
    )
    senders = jnp.arange(blocks_all, dtype=jnp.int32) // per_shard
    from_sender = (senders[:, None] == slot_ids[None, :]).astype(jnp.float32)
    placing = jnp.dot(at_offset, from_sender, precision=lax.Precision.HIGHEST).astype(jnp.bfloat16)
    packed = jnp.einsum(
        "od,drc->orc", placing, incoming, preferred_element_type=jnp.float32
    ).astype(jnp.bfloat16)
    queries_here = packed.reshape(tok_rows, q_cols)
    w_swapped = lax.ppermute(out_weight, ("ylo", "yhi"), perm=[(0, 0), (1, 2), (2, 1), (3, 3)])
    w_cols = lax.all_gather(w_swapped, "x", axis=1, tiled=True)
    w_here = lax.all_gather(w_cols, "ylo", axis=0, tiled=True)
    context, w_here = lax.optimization_barrier((context, w_here))
    ctx_keys = context[:, :kv_cols]
    ctx_values = context[:, kv_cols:]
    ctx_rows = context.shape[0]
    q_pos = shard_index * tok_rows + jnp.arange(tok_rows, dtype=jnp.int32)
    k_pos = shard_index * tok_rows - WINDOW + jnp.arange(ctx_rows, dtype=jnp.int32)
    padded_seg = jnp.concatenate([jnp.full((WINDOW,), -1, jnp.int32), segment_ids], axis=0)
    q_seg = lax.dynamic_slice_in_dim(segment_ids, shard_index * tok_rows, tok_rows, 0)
    k_seg = lax.dynamic_slice_in_dim(padded_seg, shard_index * tok_rows, ctx_rows, 0)
    heads_here = q_cols // HEAD_DIM

    def one_head(head_index):
        q_head = lax.dynamic_slice_in_dim(queries_here, head_index * HEAD_DIM, HEAD_DIM, 1)
        return attend_head(q_head, ctx_keys, ctx_values, q_pos, k_pos, q_seg, k_seg)

    per_head = lax.map(one_head, jnp.arange(heads_here, dtype=jnp.int32))
    attended = jnp.transpose(per_head, (1, 0, 2)).reshape(tok_rows, q_cols)
    h_groups = lax.all_gather(attended, "yhi", axis=1, tiled=True)
    h_here = lax.all_gather(h_groups, "c", axis=0, tiled=True)
    part = jnp.dot(h_here, w_here, preferred_element_type=jnp.float32).astype(jnp.bfloat16)
    summed = lax.psum_scatter(part, "z", scatter_dimension=1, tiled=True)
    swapped = lax.all_to_all(summed, "c", split_axis=0, concat_axis=0, tiled=True)
    return jnp.concatenate([swapped[:tok_rows], swapped[tok_rows:]], axis=1)


def solution(mesh):
    seq_count, tp_count = mesh.devices.shape
    fine = Mesh(mesh.devices.reshape(2, seq_count // 4, 2, 2, tp_count // 2), SEQ + TP)
    in_specs = (P(SEQ, TP), P(SEQ, TP), P(SEQ, TP), P(), P(), P(TP, SEQ))
    out_specs = P(SEQ, TP)
    return jax.shard_map(
        functools.partial(shards, seq_count),
        mesh=fine,
        in_specs=in_specs,
        out_specs=out_specs,
        check_vma=False,
    )
```

profile of v0, /device:TPU:1, one launch (start us, length us, event | category | flops | bytes accessed | tf_op | source)
XLA Modules:
  0.0 490.7 jit_solution(2651547205642408613)
XLA Ops:
  6.5 2.0 collective-permute-start
  9.7 1.7 pad_maximum_fusion.1
  11.5 82.0 %all-gather.8.cloned.1.call-done = bf16[768,3072]{1,0:T(8,128)(2,1)} async-done(((bf16[768,768]{1,0:T(8,128)(2,1)}), bf16[768,3072]{1,0:T(8,128)(2,1)}) %all-gather.8.cloned.1.call-update) | async-done | bytes 4718608 | tf_op jit(solution)/shard_map/all_gather | solution.py:69
  93.6 1.5 convolution_convert_fusion.1
  95.0 2.7 copy.10
  97.7 5.2 %all-to-all-start = ((bf16[16,128,768]{2,1,0:T(8,128)(2,1)}), bf16[16,128,768]{2,1,0:T(8,128)(2,1)S(1)}, u32[]{:S(2)}, u32[]{:S(2)}) async-start(bf16[16,128,768]{2,1,0:T(8,128)(2,1)} %copy.10), calls=%async_computation | async-start | bytes 6291456 | tf_op jit(solution)/shard_map/all_to_all | solution.py:55
  105.9 48.2 %all-to-all-done = bf16[16,128,768]{2,1,0:T(8,128)(2,1)S(1)} async-done(((bf16[16,128,768]{2,1,0:T(8,128)(2,1)}), bf16[16,128,768]{2,1,0:T(8,128)(2,1)S(1)}, u32[]{:S(2)}, u32[]{:S(2)}) %all-to-all-start) | async-done | bytes 3145760 | tf_op jit(solution)/shard_map/all_to_all | solution.py:55
  154.0 1.9 fusion.12
  156.9 7.8 %all-gather.6.cloned.1.call-done = bf16[8192,256]{1,0:T(8,128)(2,1)} async-done(((bf16[512,256]{1,0:T(8,128)(2,1)}), bf16[8192,256]{1,0:T(8,128)(2,1)}) %all-gather.6.cloned.1.call-update) | async-done | bytes 4194320 | tf_op jit(solution)/shard_map/all_gather | solution.py:37
  164.7 4.4 gather_fusion.1
  169.1 3.8 bitcast_select_fusion
  173.0 113.7 %all-gather.10.cloned.1.call-done = bf16[1536,3072]{1,0:T(8,128)(2,1)} async-done(((bf16[768,3072]{1,0:T(8,128)(2,1)}), bf16[1536,3072]{1,0:T(8,128)(2,1)}) %all-gather.10.cloned.1.call-update) | async-done | bytes 9437200 | tf_op jit(solution)/shard_map/all_gather | solution.py:70
  287.8 59.0 %while.13 = (s32[]{:T(128)}, bf16[6,512,128]{1,2,0:T(8,128)(2,1)}, s32[4608]{0:T(1024)}, s32[512]{0:T(512)S(1)}, s32[6]{0:T(128)S(1)}, /*index=5*/bf16[512,768]{...) while((s32[]{:T(128)}, bf16[6,512,128]{1,2,0:T(8,128)(2,1)}, ...), condition=%wide.region_4.5_spmd.clone, body=%wide.region_1.0_spmd.clone.sunk | while | flops 1238700544 | bytes 31535820 | solution.py:86
  289.0 4.2 fusion.44
  293.2 1.4 fusion.45
  294.6 2.2 fusion.46
  298.8 4.2 fusion.44
  304.4 2.2 fusion.46
  308.6 4.2 fusion.44
  314.3 2.2 fusion.46
  318.5 4.2 fusion.44
  322.7 1.4 fusion.45
  324.1 2.2 fusion.46
  328.3 4.2 fusion.44
  333.9 2.2 fusion.46
  338.1 4.2 fusion.44
  343.8 2.2 fusion.46
  346.8 32.3 %all-gather.12.cloned.1.call-done = bf16[512,1536]{0,1:T(8,128)(2,1)} async-done(((bf16[512,768]{0,1:T(8,128)(2,1)}), bf16[512,1536]{0,1:T(8,128)(2,1)}) %all-gather.12.cloned.1.call-update) | async-done | bytes 1572880 | tf_op jit(solution)/shard_map/all_gather | solution.py:88
  379.5 15.9 %all-gather.14.cloned.1.call-done = bf16[1024,1536]{0,1:T(8,128)(2,1)} async-done(((bf16[512,1536]{0,1:T(8,128)(2,1)}), bf16[1024,1536]{0,1:T(8,128)(2,1)}) %all-gather.14.cloned.1.call-update) | async-done | bytes 3145744 | tf_op jit(solution)/shard_map/all_gather | solution.py:89
  395.4 15.3 %convolution_convert_fusion = bf16[1024,3072]{1,0:T(8,128)(2,1)} fusion(bf16[1024,1536]{0,1:T(8,128)(2,1)} %all-gather.14.cloned.1.call-done, bf16[1536,3072]{1,0:T(8,128)(2,1)} %all-gather.10.cloned.1.call-done), kind=kOutput, calls=%fused_computation.18 | convolution fusion | flops 9666822144 | bytes 18874368 | tf_op jit(solution)/shard_map/dot_general | solution.py:90
  410.7 65.3 %reduce-scatter.2.cloned.1.call-done = bf16[1024,768]{1,0:T(8,128)(2,1)} async-done(((bf16[1024,3072]{1,0:T(8,128)(2,1)}), bf16[1024,768]{1,0:T(8,128)(2,1)}) %reduce-scatter.2.cloned.1.call-update) | async-done | bytes 1572880 | tf_op jit(solution)/shard_map/reduce_scatter | solution.py:91
  476.0 6.5 %all_to_all.14 = bf16[2,512,768]{2,1,0:T(8,128)(2,1)S(1)} all-to-all(bf16[2,512,768]{2,1,0:T(8,128)(2,1)} %bitcast.53), channel_id=1, replica_groups=mesh['ylo'=2,'x'=4,'c'=2,'yhi'=2,'z'=4] {'c'}, dimensions={0} | all-to-all | bytes 3145728 | tf_op jit(solution)/shard_map/all_to_all | solution.py:92
  (80 shorter events, 21.8 us)
Async XLA Ops:
  6.5 87.0 %copy-start = (bf16[512,768]{1,0:T(8,128)(2,1)S(1)}, bf16[512,768]{1,0:T(8,128)(2,1)}, u32[]{:S(2)}) copy-start(bf16[512,768]{1,0:T(8,128)(2,1)} %param.8) | copy-start | bytes 2359300
  6.5 86.9 %all-gather.8.cloned.1.call-start = ((), (), s32[]{:S(2)}) async-start(), calls=%async_computation.4 | async-start | bytes 5898240 | tf_op jit(solution)/shard_map/all_gather | solution.py:69
  6.5 2.1 collective-permute-start
  8.6 1.0 copy-start.2
  8.6 84.9 %copy-start.4 = (s32[64,2]{0,1:T(2,128)S(1)}, s32[64,2]{0,1:T(2,128)}, u32[]{:S(2)}) copy-start(s32[64,2]{0,1:T(2,128)} %param.12) | copy-start | bytes 1540
  9.6 155.1 %all-gather.6.cloned.1.call-start = ((), (), s32[]{:S(2)}) async-start(), calls=%async_computation.3 | async-start | bytes 4456448 | tf_op jit(solution)/shard_map/all_gather | solution.py:37
  11.4 275.2 %all-gather.10.cloned.1.call-start = ((), (), s32[]{:S(2)}) async-start(), calls=%async_computation.5 | async-start | bytes 14155776 | tf_op jit(solution)/shard_map/all_gather | solution.py:70
  97.7 7.1 %copy-start.3 = (s32[8192]{0:T(1024)S(1)}, s32[8192]{0:T(1024)}, u32[]{:S(2)}) copy-start(s32[8192]{0:T(1024)} %param.11) | copy-start | bytes 98308
  97.7 56.3 %all-to-all-start = ((bf16[16,128,768]{2,1,0:T(8,128)(2,1)}), bf16[16,128,768]{2,1,0:T(8,128)(2,1)S(1)}, u32[]{:S(2)}, u32[]{:S(2)}) async-start(bf16[16,128,768]{2,1,0:T(8,128)(2,1)} %copy.10), calls=%async_computation | async-start | bytes 6291456 | tf_op jit(solution)/shard_map/all_to_all | solution.py:55
  102.9 276.2 %all-gather.12.cloned.1.call-start = ((), (), s32[]{:S(2)}) async-start(), calls=%async_computation.6 | async-start | bytes 2359296 | tf_op jit(solution)/shard_map/all_gather | solution.py:88
  346.8 48.6 %all-gather.14.cloned.1.call-start = ((), (), s32[]{:S(2)}) async-start(), calls=%async_computation.7 | async-start | bytes 4718592 | tf_op jit(solution)/shard_map/all_gather | solution.py:89
  379.2 96.8 %reduce-scatter.2.cloned.1.call-start = ((), (), s32[]{:S(2)}) async-start(), calls=%async_computation.8 | async-start | bytes 7864320 | tf_op jit(solution)/shard_map/reduce_scatter | solution.py:91
  476.0 7.9 %copy-start.1 = (bf16[512,768]{1,0:T(8,128)(2,1)S(1)}, bf16[512,768]{1,0:T(8,128)(2,1)}, u32[]{:S(2)}) copy-start(bf16[512,768]{1,0:T(8,128)(2,1)} %param.8) | copy-start | bytes 2359300
Sparse Core Ops, SparseCore 0:
  9.8 83.6 all-gather.7
  95.1 69.5 all-gather.5
  166.4 120.2 all-gather.9
  346.9 32.2 all-gather.11
  380.7 14.6 all-gather.13
  410.8 65.1 reduce-scatter.1
where the time goes:
time: 491 us
  waiting for transfers between devices  365 us (74%)
  matrix products  57.6 us (12%)
  local copies, waits for them, and re-layouts  21.2 us (4%)
  other arithmetic  15.4 us (3%)
  between operations  13.6 us (3%)
  starting transfers between devices  7.67 us (2%)
  blocking collectives  6.54 us (1%)
    all_gather x1, waiting for transfers between devices, shards(): w_here = lax.all_gather(w_cols, 'ylo', axis=0, tiled=True)  114 us
    all_gather x1, waiting for transfers between devices, shards(): w_cols = lax.all_gather(w_swapped, 'x', axis=1, tiled=True)  82 us
    reduce_scatter x1, waiting for transfers between devices, shards(): summed = lax.psum_scatter(part, 'z', scatter_dimension=1, tiled=True)  65.3 us
    all_to_all x1, waiting for transfers between devices, shards(): lax.all_to_all(outgoing, SEQ, split_axis=0, concat_axis=0, tiled=True)  48.2 us
    all_gather x1, waiting for transfers between devices, shards(): h_groups = lax.all_gather(attended, 'yhi', axis=1, tiled=True)  32.3 us
    dot_general x6, matrix products, attend_head(): lax.dot_general(q_rows, k_rows, (((1,), (1,)), ((), ())), preferred_eleme...  25.4 us
    all_gather x1, waiting for transfers between devices, shards(): h_here = lax.all_gather(h_groups, 'c', axis=0, tiled=True)  15.9 us
    dot_general x1, matrix products, shards(): jnp.dot(h_here, w_here, preferred_element_type=jnp.float32)  15.3 us
  transfers between devices with their start and end apart: 8, of which 7 were waited for; matrix products, arithmetic and copies ran while one was open for 4% of the time, Pallas kernels for 0%

commit v1 on v0

--- a/solution.py
+++ b/solution.py
@@ -67,7 +67,9 @@
     queries_here = packed.reshape(tok_rows, q_cols)
     w_swapped = lax.ppermute(out_weight, ("ylo", "yhi"), perm=[(0, 0), (1, 2), (2, 1), (3, 3)])
     w_cols = lax.all_gather(w_swapped, "x", axis=1, tiled=True)
-    w_here = lax.all_gather(w_cols, "ylo", axis=0, tiled=True)
+    w_here = jnp.concatenate(
+        lax.all_to_all(jnp.stack([w_cols] * lax.axis_size("ylo")), "ylo", 0, 0), axis=0
+    )
     context, w_here = lax.optimization_barrier((context, w_here))
     ctx_keys = context[:, :kv_cols]
     ctx_values = context[:, kv_cols:]

time: 491 us -> 466 us (0.949)
  waiting for transfers between devices: 365 us -> 291 us
  starting transfers between devices: 7.67 us -> 44.6 us
  other arithmetic: 15.4 us -> 23.6 us
    all_gather x1 -> x0, waiting for transfers between devices: 114 us -> none  [shards(): w_here = lax.all_gather(w_cols, 'ylo', axis=0, tiled=True)]
    all_to_all x0 -> x1, waiting for transfers between devices: none -> 76 us  [shards(): lax.all_to_all(jnp.stack([w_cols] * lax.axis_size('ylo')), 'ylo', 0, 0)]
    all_to_all x1, waiting for transfers between devices: 48.2 us -> 0.01 us  [shards(): lax.all_to_all(outgoing, SEQ, split_axis=0, concat_axis=0, tiled=True)]
    all_to_all x1, starting transfers between devices: 5.2 us -> 34.7 us  [shards(): lax.all_to_all(outgoing, SEQ, split_axis=0, concat_axis=0, tiled=True)]
    all_gather x1, waiting for transfers between devices: 7.77 us -> 26.6 us  [shards(): kv_all = lax.all_gather(kv_local, SEQ, axis=0, tiled=True)]
    another operation x0 -> x1, other arithmetic: none -> 8.29 us  [shards(): jnp.stack([w_cols] * lax.axis_size('ylo'))]
    all_to_all x0 -> x1, starting transfers between devices: none -> 7.46 us  [shards(): lax.all_to_all(jnp.stack([w_cols] * lax.axis_size('ylo')), 'ylo', 0, 0)]
    all_gather x1, waiting for transfers between devices: 82 us -> 76 us  [shards(): w_cols = lax.all_gather(w_swapped, 'x', axis=1, tiled=True)]
  transfers between devices with their start and end apart: 8 -> 8, of which waited for: 7 -> 6; matrix products, arithmetic and copies ran while one was open for 4% -> 7% of each run, Pallas kernels for 0% -> 0%
where the time goes in v1:
time: 466 us; the launch traced here: 465 us
  waiting for transfers between devices  291 us (62%)
  matrix products  60.1 us (13%)
  starting transfers between devices  44.6 us (10%)
  other arithmetic  23.6 us (5%)
  local copies, waits for them, and re-layouts  21.8 us (5%)
  between operations  13.3 us (3%)
  blocking collectives  6.51 us (1%)
    all_to_all x1, waiting for transfers between devices, shards(): lax.all_to_all(jnp.stack([w_cols] * lax.axis_size('ylo')), 'ylo', 0, 0)  76 us
    all_gather x1, waiting for transfers between devices, shards(): w_cols = lax.all_gather(w_swapped, 'x', axis=1, tiled=True)  76 us
    reduce_scatter x1, waiting for transfers between devices, shards(): summed = lax.psum_scatter(part, 'z', scatter_dimension=1, tiled=True)  65.3 us
    all_to_all x1, starting transfers between devices, shards(): lax.all_to_all(outgoing, SEQ, split_axis=0, concat_axis=0, tiled=True)  34.7 us
    all_gather x1, waiting for transfers between devices, shards(): h_groups = lax.all_gather(attended, 'yhi', axis=1, tiled=True)  31.5 us
    all_gather x1, waiting for transfers between devices, shards(): kv_all = lax.all_gather(kv_local, SEQ, axis=0, tiled=True)  26.6 us
    dot_general x6, matrix products, attend_head(): lax.dot_general(q_rows, k_rows, (((1,), (1,)), ((), ())), preferred_eleme...  25.9 us
    all_gather x1, waiting for transfers between devices, shards(): h_here = lax.all_gather(h_groups, 'c', axis=0, tiled=True)  15.9 us
  transfers between devices with their start and end apart: 8, of which 6 were waited for; matrix products, arithmetic and copies ran while one was open for 7% of the time, Pallas kernels for 0%

profile of v1, /device:TPU:1, one launch (start us, length us, event | category | flops | bytes accessed | tf_op | source)
XLA Modules:
  0.0 464.9 jit_solution(18154866162071020420)
XLA Ops:
  6.5 2.0 collective-permute-start
  9.7 1.7 pad_maximum_fusion.2
  12.2 1.5 convolution_convert_fusion.1
  13.7 2.7 copy.10
  16.3 34.7 %all-to-all-start = ((bf16[16,128,768]{2,1,0:T(8,128)(2,1)}), bf16[16,128,768]{2,1,0:T(8,128)(2,1)}, u32[]{:S(2)}, u32[]{:S(2)}) async-start(bf16[16,128,768]{2,1,0:T(8,128)(2,1)} %copy.10), calls=%async_computation | async-start | bytes 6291456 | tf_op jit(solution)/shard_map/all_to_all | solution.py:55
  51.0 76.0 %all-gather.7.cloned.1.call-done = bf16[768,3072]{1,0:T(8,128)(2,1)} async-done(((bf16[768,768]{1,0:T(8,128)(2,1)}), bf16[768,3072]{1,0:T(8,128)(2,1)}) %all-gather.7.cloned.1.call-update) | async-done | bytes 4718608 | tf_op jit(solution)/shard_map/all_gather | solution.py:69
  127.0 8.3 %pad_maximum_fusion = bf16[2,768,3072]{2,1,0:T(8,128)(2,1)} fusion(bf16[1,768,3072]{2,1,0:T(8,128)(2,1)} %bitcast.55), kind=kLoop, calls=%fused_computation.18 | loop fusion | flops 4718592 | bytes 14155776 | tf_op jit(solution)/shard_map/stack | solution.py:71
  135.3 7.5 %all-to-all-start.1 = ((bf16[2,768,3072]{2,1,0:T(8,128)(2,1)}), bf16[2,768,3072]{2,1,0:T(8,128)(2,1)}, u32[]{:S(2)}, u32[]{:S(2)}) async-start(bf16[2,768,3072]{2,1,0:T(8,128)(2,1)} %pad_maximum_fusion), calls=%async_computation.1 | async-start | bytes 18874368 | tf_op jit(solution)/shard_map/all_to_all | solution.py:71
  145.2 3.9 fusion.12
  150.1 26.6 %all-gather.5.cloned.1.call-done = bf16[8192,256]{1,0:T(8,128)(2,1)} async-done(((bf16[512,256]{1,0:T(8,128)(2,1)}), bf16[8192,256]{1,0:T(8,128)(2,1)}) %all-gather.5.cloned.1.call-update) | async-done | bytes 4194320 | tf_op jit(solution)/shard_map/all_gather | solution.py:37
  176.7 4.5 gather_fusion.1
  181.2 3.8 bitcast_select_fusion
  185.0 76.0 %all-to-all-done.1 = bf16[2,768,3072]{2,1,0:T(8,128)(2,1)} async-done(((bf16[2,768,3072]{2,1,0:T(8,128)(2,1)}), bf16[2,768,3072]{2,1,0:T(8,128)(2,1)}, u32[]{:S(2)}, u32[]{:S(2)}) %all-to-all-start.1) | async-done | bytes 9437216 | tf_op jit(solution)/shard_map/all_to_all | solution.py:71
  261.0 1.6 fusion.31
  262.6 59.5 %while.13 = (s32[]{:T(128)}, bf16[6,512,128]{1,2,0:T(8,128)(2,1)}, s32[4608]{0:T(1024)S(1)}, s32[512]{0:T(512)S(1)}, s32[6]{0:T(128)S(1)}, /*index=5*/bf16[512,7...) while((s32[]{:T(128)}, bf16[6,512,128]{1,2,0:T(8,128)(2,1)}, ...), condition=%wide.region_4.5_spmd.clone, body=%wide.region_1.0_spmd.clone.sunk | while | flops 1238700544 | bytes 36252392 | solution.py:88
  263.8 4.3 fusion.44
  269.5 2.2 fusion.46
  273.7 4.3 fusion.44
  279.5 2.2 fusion.46
  283.6 4.3 fusion.44
  289.4 2.2 fusion.46
  293.5 4.3 fusion.44
  299.3 2.2 fusion.46
  303.5 4.3 fusion.44
  309.2 2.2 fusion.46
  313.4 4.3 fusion.44
  319.1 2.2 fusion.46
  322.2 31.5 %all-gather.9.cloned.1.call-done = bf16[512,1536]{0,1:T(8,128)(2,1)} async-done(((bf16[512,768]{0,1:T(8,128)(2,1)}), bf16[512,1536]{0,1:T(8,128)(2,1)}) %all-gather.9.cloned.1.call-update) | async-done | bytes 1572880 | tf_op jit(solution)/shard_map/all_gather | solution.py:90
  354.0 15.9 %all-gather.11.cloned.1.call-done = bf16[1024,1536]{0,1:T(8,128)(2,1)} async-done(((bf16[512,1536]{0,1:T(8,128)(2,1)}), bf16[1024,1536]{0,1:T(8,128)(2,1)}) %all-gather.11.cloned.1.call-update) | async-done | bytes 3145744 | tf_op jit(solution)/shard_map/all_gather | solution.py:91
  369.9 15.3 %convolution_convert_fusion = bf16[1024,3072]{1,0:T(8,128)(2,1)} fusion(bf16[1024,1536]{0,1:T(8,128)(2,1)} %all-gather.11.cloned.1.call-done, bf16[1536,3072]{1,0:T(8,128)(2,1)} %bitcast.15), kind=kOutput, calls=%fused_computation.19 | convolution fusion | flops 9666822144 | bytes 18874368 | tf_op jit(solution)/shard_map/dot_general | solution.py:92
  385.2 65.3 %reduce-scatter.2.cloned.1.call-done = bf16[1024,768]{1,0:T(8,128)(2,1)} async-done(((bf16[1024,3072]{1,0:T(8,128)(2,1)}), bf16[1024,768]{1,0:T(8,128)(2,1)}) %reduce-scatter.2.cloned.1.call-update) | async-done | bytes 1572880 | tf_op jit(solution)/shard_map/reduce_scatter | solution.py:93
  450.5 6.5 %all_to_all.19 = bf16[2,512,768]{2,1,0:T(8,128)(2,1)S(1)} all-to-all(bf16[2,512,768]{2,1,0:T(8,128)(2,1)} %bitcast.56), channel_id=1, replica_groups=mesh['ylo'=2,'x'=4,'c'=2,'yhi'=2,'z'=4] {'c'}, dimensions={0} | all-to-all | bytes 3145728 | tf_op jit(solution)/shard_map/all_to_all | solution.py:94
  (92 shorter events, 23.5 us)
Async XLA Ops:
  6.5 5.6 %copy-start = (bf16[512,768]{1,0:T(8,128)(2,1)S(1)}, bf16[512,768]{1,0:T(8,128)(2,1)}, u32[]{:S(2)}) copy-start(bf16[512,768]{1,0:T(8,128)(2,1)} %param.8) | copy-start | bytes 2359300
  6.5 120.5 %all-gather.7.cloned.1.call-start = ((), (), s32[]{:S(2)}) async-start(), calls=%async_computation.5 | async-start | bytes 5898240 | tf_op jit(solution)/shard_map/all_gather | solution.py:69
  6.5 2.1 collective-permute-start
  8.6 1.0 copy-start.2
  9.6 167.0 %all-gather.5.cloned.1.call-start = ((), (), s32[]{:S(2)}) async-start(), calls=%async_computation.4 | async-start | bytes 4456448 | tf_op jit(solution)/shard_map/all_gather | solution.py:37
  16.3 119.0 %all-to-all-start = ((bf16[16,128,768]{2,1,0:T(8,128)(2,1)}), bf16[16,128,768]{2,1,0:T(8,128)(2,1)}, u32[]{:S(2)}, u32[]{:S(2)}) async-start(bf16[16,128,768]{2,1,0:T(8,128)(2,1)} %copy.10), calls=%async_computation | async-start | bytes 6291456 | tf_op jit(solution)/shard_map/all_to_all | solution.py:55
  135.3 7.5 %copy-start.5 = (s32[64,2]{0,1:T(2,128)S(1)}, s32[64,2]{0,1:T(2,128)}, u32[]{:S(2)}) copy-start(s32[64,2]{0,1:T(2,128)} %param.12) | copy-start | bytes 1540
  135.3 9.3 %copy-start.4 = (s32[8192]{0:T(1024)S(1)}, s32[8192]{0:T(1024)}, u32[]{:S(2)}) copy-start(s32[8192]{0:T(1024)} %param.11) | copy-start | bytes 98308
  135.3 125.7 %all-to-all-start.1 = ((bf16[2,768,3072]{2,1,0:T(8,128)(2,1)}), bf16[2,768,3072]{2,1,0:T(8,128)(2,1)}, u32[]{:S(2)}, u32[]{:S(2)}) async-start(bf16[2,768,3072]{2,1,0:T(8,128)(2,1)} %pad_maximum_fusion), calls=%async_computation.1 | async-start | bytes 18874368 | tf_op jit(solution)/shard_map/all_to_all | solution.py:71
  142.8 210.9 %all-gather.9.cloned.1.call-start = ((), (), s32[]{:S(2)}) async-start(), calls=%async_computation.6 | async-start | bytes 2359296 | tf_op jit(solution)/shard_map/all_gather | solution.py:90
  268.1 1.4 copy-start.3
  278.0 1.4 copy-start.3
  287.9 1.4 copy-start.3
  297.9 1.4 copy-start.3
  307.8 1.4 copy-start.3
  317.7 1.4 copy-start.3
  322.1 47.7 %all-gather.11.cloned.1.call-start = ((), (), s32[]{:S(2)}) async-start(), calls=%async_computation.7 | async-start | bytes 4718592 | tf_op jit(solution)/shard_map/all_gather | solution.py:91
  353.7 96.8 %reduce-scatter.2.cloned.1.call-start = ((), (), s32[]{:S(2)}) async-start(), calls=%async_computation.8 | async-start | bytes 7864320 | tf_op jit(solution)/shard_map/reduce_scatter | solution.py:93
  450.5 7.9 %copy-start.1 = (bf16[512,768]{1,0:T(8,128)(2,1)S(1)}, bf16[512,768]{1,0:T(8,128)(2,1)}, u32[]{:S(2)}) copy-start(bf16[512,768]{1,0:T(8,128)(2,1)} %param.8) | copy-start | bytes 2359300
Sparse Core Ops, SparseCore 0:
  9.8 117.2 all-gather.6
  128.7 47.8 all-gather.4
  322.3 31.3 all-gather.8
  355.2 14.6 all-gather.10
  385.4 65.1 reduce-scatter.1
